TPU v7x, 256 devices: a whole 4x4x8 slice. The times are simulated.
256 devices in a mesh: gx: 16 (over z, x_hi), gy: 16 (over x_lo, y, core).
Axes of the slice: x: 4 (x_hi: 2, x_lo: 2; x = x_hi * 2 + x_lo), y: 4, z: 8, core: 2. Of those that a mesh axis runs over, the one named last changes fastest.
Arguments:
- tokens: bfloat16 [4096, 4096], P('gy', 'gx'), may hold values from -6 to 6
- attn_gain: bfloat16 [4096], replicated, may hold values from 0.099609375 to 1.8984375
- qkv_weight: bfloat16 [4096, 6144], P('gy', 'gx'), may hold values from -0.1875 to 0.1875
- out_weight: bfloat16 [4096, 4096], P('gx', 'gy'), may hold values from -0.09375 to 0.09375
- mlp_gain: bfloat16 [4096], replicated, may hold values from 0.099609375 to 1.8984375
- up_weight: bfloat16 [4096, 12288], P('gy', 'gx'), may hold values from -0.09375 to 0.09375
- down_weight: bfloat16 [12288, 4096], P('gx', 'gy'), may hold values from -0.0546875 to 0.0546875
- final_gain: bfloat16 [4096], replicated, may hold values from 0.099609375 to 1.8984375
- head_weight: bfloat16 [4096, 131072], P(None, ('gx', 'gy')), may hold values from -0.25 to 0.25
- kv_cache: bfloat16 [256, 4096, 256], P(('gy', 'gx')), may hold values from -40 to 40
- cache_lengths: int32 [32], replicated, may hold values from 1 to 3968, as said below
- slot_request: int32 [32], replicated, may hold values from 0 to 31, each once
Outputs:
- hidden_out: bfloat16 [4096, 4096], P('gy', 'gx')
- new_cache: bfloat16 [256, 4096, 256], P(('gy', 'gx'))
- last_norms: float32 [32], replicated
- max_logits: float32 [32], replicated
- head_input: bfloat16 [32, 4096], replicated
Inputs may be any that keep to these rules, and one draw needn't show every extreme that they name: `cache_lengths`: the longest request has exactly 3968 cached positions.
All inputs are finite; a program needn't handle non-finite values.
Results may differ from a plain program's by a relative error of at most 0.02.
The roundings to bfloat16 on the way count: a program that leaves them out, or rounds other values in their place, can miss the bound.
Values may be sent and summed in bfloat16 or wider, within the bound.
A program may use at most 128 MiB of HBM per device.

v0:
```python
import math
import jax
import jax.numpy as jnp
from jax import lax
from jax.sharding import PartitionSpec as P

HEADS = 32
KVH = 8
HD = 128
epsilon = 1e-05
negative = -1e30


def from_partner(block, axis, distance):
    count = lax.axis_size(axis)
    route = []
    for low in range(count):
        high = low | 1 << distance
        if high != low and high < count:
            route += [(low, high), (high, low)]
    return lax.ppermute(block, axis, route)


def rms_factor(row_block):
    return lax.rsqrt(jnp.mean(row_block * row_block, axis=-1, keepdims=True) + epsilon)


def gather_features(shard_rows):
    return lax.all_gather(shard_rows, "gx", axis=1, tiled=True)


def rows_product(left_rows, weight_shard):
    return jnp.dot(
        left_rows,
        lax.all_gather(weight_shard, "gy", axis=0, tiled=True),
        preferred_element_type=jnp.float32,
    )


def columns_product(left_rows, weight_shard):
    return jnp.dot(
        left_rows,
        lax.all_gather(weight_shard, "gy", axis=1, tiled=True),
        preferred_element_type=jnp.float32,
    )


def pair_swap(values):
    return from_partner(values, "gx", KVH.bit_length() - 1)


def scatter_partials(partial_terms):
    return lax.psum_scatter(
        partial_terms.astype(jnp.bfloat16), "gx", scatter_dimension=1, tiled=True
    ).astype(jnp.float32)


def merge_block(carried, scores, value_rows):
    row_max, running, numerator = carried
    new_max = jnp.maximum(row_max, jnp.max(scores, axis=1, keepdims=True))
    factor = jnp.exp(row_max - new_max)
    weights = jnp.exp(scores - new_max)
    running = running * factor + jnp.sum(weights, axis=1, keepdims=True)
    numerator = numerator * factor + jnp.dot(
        weights.astype(jnp.bfloat16), value_rows, preferred_element_type=jnp.float32
    )
    return (new_max, running, numerator)


def attend_cache(group_cols, cache_rows, length, new_rows):
    per_group = HEADS // KVH
    scaling = 1.0 / math.sqrt(HD)
    query_rows = per_group * new_rows
    queries = (
        group_cols[:, : per_group * HD]
        .reshape(new_rows, per_group, HD)
        .transpose(1, 0, 2)
        .reshape(query_rows, HD)
    )
    key_new = group_cols[:, per_group * HD : (per_group + 1) * HD]
    value_new = group_cols[:, (per_group + 1) * HD :]
    block_len = min(512, cache_rows.shape[0])

    def visit_block(step_index, carried):
        offset = step_index * block_len
        block_rows = lax.dynamic_slice_in_dim(cache_rows, offset, block_len, 0)
        scores = (
            jnp.dot(queries, block_rows[:, :HD].T, preferred_element_type=jnp.float32) * scaling
        )
        positions = offset + jnp.arange(block_len)
        scores = jnp.where(positions[None, :] < length, scores, negative)
        return merge_block(carried, scores, block_rows[:, HD:])

    initial = (
        jnp.full((query_rows, 1), negative, jnp.float32),
        jnp.zeros((query_rows, 1), jnp.float32),
        jnp.zeros((query_rows, HD), jnp.float32),
    )
    block_count = (length + block_len - 1) // block_len
    carried = lax.fori_loop(0, block_count, visit_block, initial)
    new_scores = jnp.dot(queries, key_new.T, preferred_element_type=jnp.float32) * scaling
    causal = jnp.arange(new_rows)[None, :] <= (jnp.arange(query_rows) % new_rows)[:, None]
    new_scores = jnp.where(causal, new_scores, negative)
    row_max, running, numerator = merge_block(carried, new_scores, value_new)
    attended = (numerator / running).astype(jnp.bfloat16)
    attended = (
        attended.reshape(per_group, new_rows, HD)
        .transpose(1, 0, 2)
        .reshape(new_rows, per_group * HD)
    )
    fresh = jnp.concatenate([key_new, value_new], axis=1)
    appended = lax.dynamic_update_slice(cache_rows, fresh, (length, jnp.zeros((), jnp.int32)))
    return (attended, appended)


def local(
    tokens,
    attn_gain,
    qkv_weight,
    out_weight,
    mlp_gain,
    up_weight,
    down_weight,
    final_gain,
    head_weight,
    kv_cache,
    cache_lengths,
    slot_request,
):
    gx_count = lax.axis_size("gx")
    gy_count = lax.axis_size("gy")
    copies = gx_count // KVH
    gx_place = lax.axis_index("gx")
    copy_index = gx_place // KVH
    slot_index = lax.axis_index("gy") * copies + copy_index
    new_rows = tokens.shape[0] // copies
    feature_cols = tokens.shape[1]
    gathered_tokens = gather_features(tokens)
    tokens_f32 = gathered_tokens.astype(jnp.float32)
    normed = (tokens_f32 * rms_factor(tokens_f32) * attn_gain.astype(jnp.float32)).astype(
        jnp.bfloat16
    )
    projected = rows_product(normed, qkv_weight).astype(jnp.bfloat16)
    own_half = lax.dynamic_slice_in_dim(projected, copy_index * new_rows, new_rows, 0)
    sent_rows = lax.dynamic_slice_in_dim(projected, (1 - copy_index) * new_rows, new_rows, 0)
    received = pair_swap(sent_rows)
    group_cols = jnp.where(
        copy_index == 0,
        jnp.concatenate([own_half, received], axis=1),
        jnp.concatenate([received, own_half], axis=1),
    )
    length = cache_lengths[slot_request[slot_index]]
    attended, appended = attend_cache(group_cols, kv_cache[0], length, new_rows)
    new_cache = appended[None]
    half_width = attended.shape[1] // 2
    kept_half = lax.dynamic_slice_in_dim(attended, copy_index * half_width, half_width, 1)
    handed = lax.dynamic_slice_in_dim(attended, (1 - copy_index) * half_width, half_width, 1)
    returned = pair_swap(handed)
    attention_rows = jnp.where(
        copy_index == 0,
        jnp.concatenate([kept_half, returned], axis=0),
        jnp.concatenate([returned, kept_half], axis=0),
    )
    attention_terms = columns_product(attention_rows, out_weight)
    middle = (tokens.astype(jnp.float32) + scatter_partials(attention_terms)).astype(jnp.bfloat16)
    middle_full = gather_features(middle)
    middle_f32 = middle_full.astype(jnp.float32)
    mlp_input = (middle_f32 * rms_factor(middle_f32) * mlp_gain.astype(jnp.float32)).astype(
        jnp.bfloat16
    )
    up_values = rows_product(mlp_input, up_weight)
    rectified = jnp.maximum(up_values, 0.0)
    activation = (rectified * rectified).astype(jnp.bfloat16)
    down_terms = columns_product(activation, down_weight)
    hidden_out = (middle.astype(jnp.float32) + scatter_partials(down_terms)).astype(jnp.bfloat16)
    final_rows = hidden_out.reshape(copies, new_rows, feature_cols)[:, new_rows - 1, :]
    every_last = lax.all_gather(final_rows, ("gx", "gy"), axis=0, tiled=True)
    slot_rows = every_last.reshape(gx_count, gy_count, copies, feature_cols).transpose(1, 2, 0, 3)
    slot_rows = slot_rows.reshape(gy_count * copies, gx_count * feature_cols).astype(jnp.float32)
    mean_square = jnp.mean(slot_rows * slot_rows, axis=1)
    last_norms = jnp.sqrt(mean_square)
    head_input = (
        slot_rows * lax.rsqrt(mean_square + epsilon)[:, None] * final_gain.astype(jnp.float32)
    ).astype(jnp.bfloat16)
    logits = jnp.dot(head_input, head_weight, preferred_element_type=jnp.float32)
    max_logits = lax.pmax(jnp.max(logits, axis=1), ("gx", "gy"))
    return (hidden_out, new_cache, last_norms, max_logits, head_input)


def solution(mesh):
    in_specs = (
        P("gy", "gx"),
        P(),
        P("gy", "gx"),
        P("gx", "gy"),
        P(),
        P("gy", "gx"),
        P("gx", "gy"),
        P(),
        P(None, ("gx", "gy")),
        P(("gy", "gx"), None, None),
        P(),
        P(),
    )
    out_specs = (P("gy", "gx"), P(("gy", "gx"), None, None), P(), P(), P())
    return jax.shard_map(local, mesh=mesh, in_specs=in_specs, out_specs=out_specs, check_vma=False)
```

profile of v0, /device:TPU:1, one launch (start us, length us, event | category | flops | bytes accessed | tf_op | source)
XLA Modules:
  0.0 957.5 jit_solution(2756551729727596490)
XLA Ops:
  13.4 81.3 %all-gather.8.cloned.1.call-done = bf16[256,4096]{1,0:T(8,128)(2,1)} async-done(((bf16[256,256]{1,0:T(8,128)(2,1)}), bf16[256,4096]{1,0:T(8,128)(2,1)}) %all-gather.8.cloned.1.call-update) | async-done | bytes 2097168 | tf_op jit(solution)/shard_map/all_gather | solution.py:29
  94.6 2.1 fusion.8
  96.7 39.1 %all-gather.10.cloned.1.call-done = bf16[4096,384]{1,0:T(8,128)(2,1)} async-done(((bf16[256,384]{1,0:T(8,128)(2,1)}), bf16[4096,384]{1,0:T(8,128)(2,1)}) %all-gather.10.cloned.1.call-update) | async-done | bytes 3145744 | tf_op jit(solution)/shard_map/all_gather | solution.py:35
  135.8 3.8 fusion.31
  139.7 5.5 collective-permute-start
  145.2 2.7 collective-permute-done
  148.0 1.5 fusion.58
  149.6 4.9 while.14
  156.2 1.2 fusion.36
  157.6 5.5 collective-permute-start.1
  163.2 14.0 %all-gather.12.cloned.1.call-done = bf16[256,4096]{1,0:T(8,128)(2,1)} async-done(((bf16[256,256]{1,0:T(8,128)(2,1)}), bf16[256,4096]{1,0:T(8,128)(2,1)}) %all-gather.12.cloned.1.call-update) | async-done | bytes 2097168 | tf_op jit(solution)/shard_map/all_gather | solution.py:43
  177.2 3.7 convolution_convert_fusion
  180.9 205.0 %reduce-scatter.3.cloned.1.call-done = bf16[256,256]{1,0:T(8,128)(2,1)} async-done(((bf16[256,4096]{1,0:T(8,128)(2,1)}), bf16[256,256]{1,0:T(8,128)(2,1)}) %reduce-scatter.3.cloned.1.call-update) | async-done | bytes 131088 | tf_op jit(solution)/shard_map/reduce_scatter | solution.py:53
  385.9 1.6 add_convert_fusion.1
  388.9 83.5 %all-gather.14.cloned.1.call-done = bf16[256,4096]{1,0:T(8,128)(2,1)} async-done(((bf16[256,256]{1,0:T(8,128)(2,1)}), bf16[256,4096]{1,0:T(8,128)(2,1)}) %all-gather.14.cloned.1.call-update) | async-done | bytes 2097168 | tf_op jit(solution)/shard_map/all_gather | solution.py:29
  472.4 2.1 fusion.11
  474.5 45.9 %all-gather.16.cloned.1.call-done = bf16[4096,768]{1,0:T(8,128)(2,1)} async-done(((bf16[256,768]{1,0:T(8,128)(2,1)}), bf16[4096,768]{1,0:T(8,128)(2,1)}) %all-gather.16.cloned.1.call-update) | async-done | bytes 6291472 | tf_op jit(solution)/shard_map/all_gather | solution.py:35
  520.4 58.7 %all-gather.18.cloned.1.call-done = bf16[768,4096]{1,0:T(8,128)(2,1)} async-done(((bf16[768,256]{1,0:T(8,128)(2,1)}), bf16[768,4096]{1,0:T(8,128)(2,1)}) %all-gather.18.cloned.1.call-update) | async-done | bytes 6291472 | tf_op jit(solution)/shard_map/all_gather | solution.py:43
  579.0 11.1 %convolution_convert_fusion.1 = bf16[256,4096]{1,0:T(8,128)(2,1)} fusion(bf16[768,4096]{1,0:T(8,128)(2,1)} %all-gather.18.cloned.1.call-done, bf16[4096,768]{1,0:T(8,128)(2,1)} %all-gather.16.cloned.1.call-done, bf16[256,4096]{1,0:T(8,128)(2,1)} %all-gather.14.cloned.1.call-done, f32[4096]{0:T(1024)S(1)} %convert_element_type.90, f32[256]{0:T(256)S(1)} %add_rsqrt_fusion.1), kind=kOutput, calls=%fused_computation.18 | convolution fusion | flops 3227058176 | bytes 16794624 | tf_op jit(solution)/shard_map/dot_general | solution.py:41
  593.0 201.4 %reduce-scatter.5.cloned.1.call-done = bf16[256,256]{1,0:T(8,128)(2,1)} async-done(((bf16[256,4096]{1,0:T(8,128)(2,1)}), bf16[256,256]{1,0:T(8,128)(2,1)}) %reduce-scatter.5.cloned.1.call-update) | async-done | bytes 131088 | tf_op jit(solution)/shard_map/reduce_scatter | solution.py:53
  795.4 72.9 %all-gather = bf16[512,1,256]{2,1,0:T(2,128)(2,1)S(1)} all-gather(bf16[2,1,256]{2,1,0:T(2,128)(2,1)S(1)} %slice.26), channel_id=2, replica_groups=mesh['gx'=16,'gy'=16] {'gx','gy'}, dimensions={0}, use_global_device_ids=true | all-gather | bytes 263168 | tf_op jit(solution)/shard_map/all_gather | solution.py:177
  868.3 2.2 convert_reduce_fusion
  871.9 3.2 convolution_reduce_fusion
  875.8 74.3 %pmax.7 = f32[32]{0:T(128)} all-reduce(f32[32]{0:T(128)S(1)} %convolution_reduce_fusion), channel_id=1, replica_groups=mesh['gx'=16,'gy'=16] {'gx','gy'}, use_global_device_ids=true, to_apply=%region_13.14 | all-reduce | flops 32 | bytes 256 | tf_op jit(solution)/shard_map/pmax | solution.py:186
  (96 shorter events, 16.0 us)
Async XLA Ops:
  7.2 6.1 copy-start.7
  7.2 4.9 copy-start.11
  7.2 2.3 copy-start.10
  7.2 87.4 %all-gather.8.cloned.1.call-start = ((), (), s32[]{:S(2)}) async-start(), calls=%async_computation.2 | async-start | bytes 2228224 | tf_op jit(solution)/shard_map/all_gather | solution.py:29
  7.9 127.9 %all-gather.10.cloned.1.call-start = ((), (), s32[]{:S(2)}) async-start(), calls=%async_computation.3 | async-start | bytes 3342336 | tf_op jit(solution)/shard_map/all_gather | solution.py:35
  8.7 168.5 %all-gather.12.cloned.1.call-start = ((), (), s32[]{:S(2)}) async-start(), calls=%async_computation.4 | async-start | bytes 2228224 | tf_op jit(solution)/shard_map/all_gather | solution.py:43
  9.4 376.5 %reduce-scatter.3.cloned.1.call-start = ((), (), s32[]{:S(2)}) async-start(), calls=%async_computation.5 | async-start | bytes 2228224 | tf_op jit(solution)/shard_map/reduce_scatter | solution.py:53
  96.7 52.8 %copy-start.1 = (bf16[1,4096,256]{2,1,0:T(8,128)(2,1)S(1)}, bf16[1,4096,256]{2,1,0:T(8,128)(2,1)}, u32[]{:S(2)}) copy-start(bf16[1,4096,256]{2,1,0:T(8,128)(2,1)} %param.23) | copy-start | bytes 6291460
  139.7 8.2 collective-permute-start
  148.0 1.6 copy-start.4
  157.6 19.5 %collective-permute-start.1 = (bf16[128,256]{0,1:T(8,128)(2,1)S(1)}, bf16[128,256]{0,1:T(8,128)(2,1)S(1)}, u32[]{:S(2)}, u32[]{:S(2)}) collective-permute-start(bf16[128,256]{0,1:T(8,128)(2,1)S(1)} %get-tuple-element.80), channel_id=1, source_target_pairs={{0,128},{128,0},{16,144},{144,16},{32,160},{160,32},{48,176},{176,... | collective-permute-start | bytes 196616 | tf_op jit(solution)/shard_map/ppermute | solution.py:21
  177.1 208.7 %copy-start.5 = (bf16[256,256]{1,0:T(8,128)(2,1)S(1)}, bf16[256,256]{1,0:T(8,128)(2,1)}, u32[]{:S(2)}) copy-start(bf16[256,256]{1,0:T(8,128)(2,1)} %param.14) | copy-start | bytes 393220
  177.1 211.7 %copy-start.8 = (bf16[4096]{0:T(1024)(128)(2,1)S(1)}, bf16[4096]{0:T(1024)(128)(2,1)}, u32[]{:S(2)}) copy-start(bf16[4096]{0:T(1024)(128)(2,1)} %param.18) | copy-start | bytes 24580
  180.9 291.5 %all-gather.14.cloned.1.call-start = ((), (), s32[]{:S(2)}) async-start(), calls=%async_computation.6 | async-start | bytes 2228224 | tf_op jit(solution)/shard_map/all_gather | solution.py:29
  387.5 132.8 %all-gather.16.cloned.1.call-start = ((), (), s32[]{:S(2)}) async-start(), calls=%async_computation.7 | async-start | bytes 6684672 | tf_op jit(solution)/shard_map/all_gather | solution.py:35
  388.1 190.9 %all-gather.18.cloned.1.call-start = ((), (), s32[]{:S(2)}) async-start(), calls=%async_computation.8 | async-start | bytes 6684672 | tf_op jit(solution)/shard_map/all_gather | solution.py:43
  388.8 405.6 %reduce-scatter.5.cloned.1.call-start = ((), (), s32[]{:S(2)}) async-start(), calls=%async_computation.9 | async-start | bytes 2228224 | tf_op jit(solution)/shard_map/reduce_scatter | solution.py:53
  474.5 117.0 %copy-start.9 = (bf16[4096]{0:T(1024)(128)(2,1)S(1)}, bf16[4096]{0:T(1024)(128)(2,1)}, u32[]{:S(2)}) copy-start(bf16[4096]{0:T(1024)(128)(2,1)} %param.21) | copy-start | bytes 24580
  474.5 320.0 %copy-start.2 = (bf16[256,256]{1,0:T(8,128)(2,1)S(1)}, bf16[256,256]{1,0:T(8,128)(2,1)}, u32[]{:S(2)}) copy-start(bf16[256,256]{1,0:T(8,128)(2,1)} %add_convert_fusion.1) | copy-start | bytes 393220
  795.4 79.8 %copy-start.6 = (bf16[256,256]{1,0:T(8,128)(2,1)}, bf16[256,256]{1,0:T(8,128)(2,1)S(1)}, u32[]{:S(2)}) copy-start(bf16[256,256]{1,0:T(8,128)(2,1)S(1)} %add_convert_fusion) | copy-start | bytes 393220
  871.9 78.7 %copy-start.3 = (bf16[32,4096]{1,0:T(8,128)(2,1)}, bf16[32,4096]{1,0:T(8,128)(2,1)S(1)}, u32[]{:S(2)}) copy-start(bf16[32,4096]{1,0:T(8,128)(2,1)S(1)} %multiply_convert_fusion) | copy-start | bytes 786436
  875.8 74.9 %copy-start = (bf16[1,4096,256]{2,1,0:T(8,128)(2,1)}, bf16[1,4096,256]{2,1,0:T(8,128)(2,1)S(1)}, u32[]{:S(2)}) copy-start(bf16[1,4096,256]{2,1,0:T(8,128)(2,1)S(1)} %dynamic_update_slice.4) | copy-start | bytes 6291460
Sparse Core Ops, SparseCore 0:
  10.5 84.1 all-gather.7
  96.5 39.2 all-gather.9
  137.6 39.5 all-gather.11
  181.5 204.3 reduce-scatter.2
  388.8 83.5 all-gather.13
  474.1 46.2 all-gather.15
  522.1 56.8 all-gather.17
  590.3 204.0 reduce-scatter.4
where the time goes:
time: 958 us; the launch traced here: 957 us
  waiting for transfers between devices  735 us (77%)
  blocking collectives  147 us (15%)
  matrix products  26.7 us (3%)
  between operations  19.1 us (2%)
  other arithmetic  13.5 us (1%)
  starting transfers between devices  11.4 us (1%)
    reduce_scatter x2, waiting for transfers between devices, scatter_partials(): lax.psum_scatter(partial_terms.astype(jnp.bfloat16), 'gx', scatter_dimens...  406 us
    all_gather x2, waiting for transfers between devices, gather_features(): return lax.all_gather(shard_rows, 'gx', axis=1, tiled=True)  165 us
    all_gather x2, waiting for transfers between devices, rows_product(): lax.all_gather(weight_shard, 'gy', axis=0, tiled=True)  84.9 us
    pmax x1, blocking collectives, local(): max_logits = lax.pmax(jnp.max(logits, axis=1), ('gx', 'gy'))  74.3 us
    all_gather x1, blocking collectives, local(): every_last = lax.all_gather(final_rows, ('gx', 'gy'), axis=0, tiled=True)  72.9 us
    all_gather x2, waiting for transfers between devices, columns_product(): lax.all_gather(weight_shard, 'gy', axis=1, tiled=True)  72.7 us
  transfers between devices with their start and end apart: 10, of which 9 were waited for; matrix products, arithmetic and copies ran while one was open for 2% of the time, Pallas kernels for 0%

commit v1 on v0

--- a/solution.py
+++ b/solution.py
@@ -174,7 +174,15 @@
     down_terms = columns_product(activation, down_weight)
     hidden_out = (middle.astype(jnp.float32) + scatter_partials(down_terms)).astype(jnp.bfloat16)
     final_rows = hidden_out.reshape(copies, new_rows, feature_cols)[:, new_rows - 1, :]
-    every_last = lax.all_gather(final_rows, ("gx", "gy"), axis=0, tiled=True)
+    every_last = jnp.concatenate(
+        lax.all_to_all(
+            jnp.stack(lax.psum(1, ("gx", "gy")) * [final_rows]),
+            axis_name=("gx", "gy"),
+            split_axis=0,
+            concat_axis=0,
+        ),
+        axis=0,
+    )
     slot_rows = every_last.reshape(gx_count, gy_count, copies, feature_cols).transpose(1, 2, 0, 3)
     slot_rows = slot_rows.reshape(gy_count * copies, gx_count * feature_cols).astype(jnp.float32)
     mean_square = jnp.mean(slot_rows * slot_rows, axis=1)

time: 958 us -> 912 us (0.952)
  blocking collectives: 147 us -> 72.6 us
  waiting for transfers between devices: 735 us -> 750 us
  starting transfers between devices: 11.4 us -> 26.4 us
    all_gather x1 -> x0, blocking collectives: 72.9 us -> none  [local(): every_last = lax.all_gather(final_rows, ('gx', 'gy'), axis=0, tiled=True)]
    all_to_all x0 -> x1, starting transfers between devices: none -> 15 us  [local(): lax.all_to_all(jnp.stack(lax.psum(1, ('gx', 'gy')) * [final_rows]), axis_...]
    all_to_all x0 -> x1, waiting for transfers between devices: none -> 12.5 us  [local(): lax.all_to_all(jnp.stack(lax.psum(1, ('gx', 'gy')) * [final_rows]), axis_...]
  transfers between devices with their start and end apart: 10 -> 11, of which waited for: 9 -> 10; matrix products, arithmetic and copies ran while one was open for 2% -> 2% of each run, Pallas kernels for 0% -> 0%
where the time goes in v1:
time: 912 us
  waiting for transfers between devices  750 us (82%)
  blocking collectives  72.6 us (8%)
  matrix products  26.7 us (3%)
  starting transfers between devices  26.4 us (3%)
  between operations  19.1 us (2%)
  other arithmetic  11.5 us (1%)
    reduce_scatter x2, waiting for transfers between devices, scatter_partials(): lax.psum_scatter(partial_terms.astype(jnp.bfloat16), 'gx', scatter_dimens...  409 us
    all_gather x2, waiting for transfers between devices, gather_features(): return lax.all_gather(shard_rows, 'gx', axis=1, tiled=True)  165 us
    all_gather x2, waiting for transfers between devices, rows_product(): lax.all_gather(weight_shard, 'gy', axis=0, tiled=True)  84.9 us
    all_gather x2, waiting for transfers between devices, columns_product(): lax.all_gather(weight_shard, 'gy', axis=1, tiled=True)  72.7 us
    pmax x1, blocking collectives, local(): max_logits = lax.pmax(jnp.max(logits, axis=1), ('gx', 'gy'))  72.6 us
  transfers between devices with their start and end apart: 11, of which 10 were waited for; matrix products, arithmetic and copies ran while one was open for 2% of the time, Pallas kernels for 0%

profile of v1, /device:TPU:1, one launch (start us, length us, event | category | flops | bytes accessed | tf_op | source)
XLA Modules:
  0.0 911.8 jit_solution(16123884641705987061)
XLA Ops:
  13.4 81.3 %all-gather.7.cloned.1.call-done = bf16[256,4096]{1,0:T(8,128)(2,1)} async-done(((bf16[256,256]{1,0:T(8,128)(2,1)}), bf16[256,4096]{1,0:T(8,128)(2,1)}) %all-gather.7.cloned.1.call-update) | async-done | bytes 2097168 | tf_op jit(solution)/shard_map/all_gather | solution.py:29
  94.6 2.1 fusion.8
  96.7 39.1 %all-gather.9.cloned.1.call-done = bf16[4096,384]{1,0:T(8,128)(2,1)} async-done(((bf16[256,384]{1,0:T(8,128)(2,1)}), bf16[4096,384]{1,0:T(8,128)(2,1)}) %all-gather.9.cloned.1.call-update) | async-done | bytes 3145744 | tf_op jit(solution)/shard_map/all_gather | solution.py:35
  135.8 3.8 fusion.31
  139.7 5.5 collective-permute-start
  145.2 2.7 collective-permute-done
  148.0 1.5 fusion.58
  149.6 4.9 while.14
  156.2 1.2 fusion.36
  157.6 5.5 collective-permute-start.1
  163.2 14.0 %all-gather.11.cloned.1.call-done = bf16[256,4096]{1,0:T(8,128)(2,1)} async-done(((bf16[256,256]{1,0:T(8,128)(2,1)}), bf16[256,4096]{1,0:T(8,128)(2,1)}) %all-gather.11.cloned.1.call-update) | async-done | bytes 2097168 | tf_op jit(solution)/shard_map/all_gather | solution.py:43
  177.2 3.7 convolution_convert_fusion
  180.9 205.0 %reduce-scatter.3.cloned.1.call-done = bf16[256,256]{1,0:T(8,128)(2,1)} async-done(((bf16[256,4096]{1,0:T(8,128)(2,1)}), bf16[256,256]{1,0:T(8,128)(2,1)}) %reduce-scatter.3.cloned.1.call-update) | async-done | bytes 131088 | tf_op jit(solution)/shard_map/reduce_scatter | solution.py:53
  385.9 1.6 add_convert_fusion.1
  388.9 83.5 %all-gather.13.cloned.1.call-done = bf16[256,4096]{1,0:T(8,128)(2,1)} async-done(((bf16[256,256]{1,0:T(8,128)(2,1)}), bf16[256,4096]{1,0:T(8,128)(2,1)}) %all-gather.13.cloned.1.call-update) | async-done | bytes 2097168 | tf_op jit(solution)/shard_map/all_gather | solution.py:29
  472.4 2.1 fusion.11
  474.5 45.9 %all-gather.15.cloned.1.call-done = bf16[4096,768]{1,0:T(8,128)(2,1)} async-done(((bf16[256,768]{1,0:T(8,128)(2,1)}), bf16[4096,768]{1,0:T(8,128)(2,1)}) %all-gather.15.cloned.1.call-update) | async-done | bytes 6291472 | tf_op jit(solution)/shard_map/all_gather | solution.py:35
  520.4 58.7 %all-gather.17.cloned.1.call-done = bf16[768,4096]{1,0:T(8,128)(2,1)} async-done(((bf16[768,256]{1,0:T(8,128)(2,1)}), bf16[768,4096]{1,0:T(8,128)(2,1)}) %all-gather.17.cloned.1.call-update) | async-done | bytes 6291472 | tf_op jit(solution)/shard_map/all_gather | solution.py:43
  579.0 11.1 %convolution_convert_fusion.1 = bf16[256,4096]{1,0:T(8,128)(2,1)} fusion(bf16[768,4096]{1,0:T(8,128)(2,1)} %all-gather.17.cloned.1.call-done, bf16[4096,768]{1,0:T(8,128)(2,1)} %all-gather.15.cloned.1.call-done, bf16[256,4096]{1,0:T(8,128)(2,1)} %all-gather.13.cloned.1.call-done, f32[4096]{0:T(1024)S(1)} %convert_element_type.90, f32[256]{0:T(256)S(1)} %add_rsqrt_fusion.1), kind=kOutput, calls=%fused_computation.18 | convolution fusion | flops 3227058176 | bytes 16794624 | tf_op jit(solution)/shard_map/dot_general | solution.py:41
  590.2 204.2 %reduce-scatter.5.cloned.1.call-done = bf16[256,256]{1,0:T(8,128)(2,1)} async-done(((bf16[256,4096]{1,0:T(8,128)(2,1)}), bf16[256,256]{1,0:T(8,128)(2,1)}) %reduce-scatter.5.cloned.1.call-update) | async-done | bytes 131088 | tf_op jit(solution)/shard_map/reduce_scatter | solution.py:53
  796.3 15.0 %all-to-all-start = ((bf16[256,2,256]{2,1,0:T(2,128)(2,1)}), bf16[256,2,256]{2,1,0:T(2,128)(2,1)S(1)}, u32[]{:S(2)}, u32[]{:S(2)}) async-start(bf16[256,2,256]{2,1,0:T(2,128)(2,1)} %stack.3), calls=%async_computation.2 | async-start | bytes 524288 | tf_op jit(solution)/shard_map/all_to_all | solution.py:178
  814.1 12.5 %all-to-all-done = bf16[256,2,256]{2,1,0:T(2,128)(2,1)S(1)} async-done(((bf16[256,2,256]{2,1,0:T(2,128)(2,1)}), bf16[256,2,256]{2,1,0:T(2,128)(2,1)S(1)}, u32[]{:S(2)}, u32[]{:S(2)}) %all-to-all-start) | async-done | bytes 262176 | tf_op jit(solution)/shard_map/all_to_all | solution.py:178
  827.8 3.2 convolution_reduce_fusion
  831.7 72.6 %pmax.7 = f32[32]{0:T(128)} all-reduce(f32[32]{0:T(128)S(1)} %convolution_reduce_fusion), channel_id=1, replica_groups=mesh['gx'=16,'gy'=16] {'gx','gy'}, use_global_device_ids=true, to_apply=%region_13.14 | all-reduce | flops 32 | bytes 256 | tf_op jit(solution)/shard_map/pmax | solution.py:194
  (101 shorter events, 16.9 us)
Async XLA Ops:
  7.2 6.1 copy-start.7
  7.2 4.9 copy-start.11
  7.2 2.3 copy-start.10
  7.2 87.4 %all-gather.7.cloned.1.call-start = ((), (), s32[]{:S(2)}) async-start(), calls=%async_computation.3 | async-start | bytes 2228224 | tf_op jit(solution)/shard_map/all_gather | solution.py:29
  7.9 127.9 %all-gather.9.cloned.1.call-start = ((), (), s32[]{:S(2)}) async-start(), calls=%async_computation.4 | async-start | bytes 3342336 | tf_op jit(solution)/shard_map/all_gather | solution.py:35
  8.7 168.5 %all-gather.11.cloned.1.call-start = ((), (), s32[]{:S(2)}) async-start(), calls=%async_computation.5 | async-start | bytes 2228224 | tf_op jit(solution)/shard_map/all_gather | solution.py:43
  9.4 376.5 %reduce-scatter.3.cloned.1.call-start = ((), (), s32[]{:S(2)}) async-start(), calls=%async_computation.6 | async-start | bytes 2228224 | tf_op jit(solution)/shard_map/reduce_scatter | solution.py:53
  96.7 52.8 %copy-start.1 = (bf16[1,4096,256]{2,1,0:T(8,128)(2,1)S(1)}, bf16[1,4096,256]{2,1,0:T(8,128)(2,1)}, u32[]{:S(2)}) copy-start(bf16[1,4096,256]{2,1,0:T(8,128)(2,1)} %param.23) | copy-start | bytes 6291460
  139.7 8.2 collective-permute-start
  148.0 1.6 copy-start.4
  157.6 19.5 %collective-permute-start.1 = (bf16[128,256]{0,1:T(8,128)(2,1)S(1)}, bf16[128,256]{0,1:T(8,128)(2,1)S(1)}, u32[]{:S(2)}, u32[]{:S(2)}) collective-permute-start(bf16[128,256]{0,1:T(8,128)(2,1)S(1)} %get-tuple-element.78), channel_id=1, source_target_pairs={{0,128},{128,0},{16,144},{144,16},{32,160},{160,32},{48,176},{176,... | collective-permute-start | bytes 196616 | tf_op jit(solution)/shard_map/ppermute | solution.py:21
  177.1 208.7 %copy-start.5 = (bf16[256,256]{1,0:T(8,128)(2,1)S(1)}, bf16[256,256]{1,0:T(8,128)(2,1)}, u32[]{:S(2)}) copy-start(bf16[256,256]{1,0:T(8,128)(2,1)} %param.14) | copy-start | bytes 393220
  177.1 211.7 %copy-start.8 = (bf16[4096]{0:T(1024)(128)(2,1)S(1)}, bf16[4096]{0:T(1024)(128)(2,1)}, u32[]{:S(2)}) copy-start(bf16[4096]{0:T(1024)(128)(2,1)} %param.18) | copy-start | bytes 24580
  180.9 291.5 %all-gather.13.cloned.1.call-start = ((), (), s32[]{:S(2)}) async-start(), calls=%async_computation.7 | async-start | bytes 2228224 | tf_op jit(solution)/shard_map/all_gather | solution.py:29
  387.5 132.8 %all-gather.15.cloned.1.call-start = ((), (), s32[]{:S(2)}) async-start(), calls=%async_computation.8 | async-start | bytes 6684672 | tf_op jit(solution)/shard_map/all_gather | solution.py:35
  388.1 190.9 %all-gather.17.cloned.1.call-start = ((), (), s32[]{:S(2)}) async-start(), calls=%async_computation.9 | async-start | bytes 6684672 | tf_op jit(solution)/shard_map/all_gather | solution.py:43
  388.8 405.6 %reduce-scatter.5.cloned.1.call-start = ((), (), s32[]{:S(2)}) async-start(), calls=%async_computation.10 | async-start | bytes 2228224 | tf_op jit(solution)/shard_map/reduce_scatter | solution.py:53
  474.5 320.0 %copy-start.2 = (bf16[256,256]{1,0:T(8,128)(2,1)S(1)}, bf16[256,256]{1,0:T(8,128)(2,1)}, u32[]{:S(2)}) copy-start(bf16[256,256]{1,0:T(8,128)(2,1)} %add_convert_fusion.1) | copy-start | bytes 393220
  590.2 222.4 %copy-start.9 = (bf16[4096]{0:T(1024)(128)(2,1)S(1)}, bf16[4096]{0:T(1024)(128)(2,1)}, u32[]{:S(2)}) copy-start(bf16[4096]{0:T(1024)(128)(2,1)} %param.21) | copy-start | bytes 24580
  795.4 0.9 copy-start.6
  796.3 30.3 %all-to-all-start = ((bf16[256,2,256]{2,1,0:T(2,128)(2,1)}), bf16[256,2,256]{2,1,0:T(2,128)(2,1)S(1)}, u32[]{:S(2)}, u32[]{:S(2)}) async-start(bf16[256,2,256]{2,1,0:T(2,128)(2,1)} %stack.3), calls=%async_computation.2 | async-start | bytes 524288 | tf_op jit(solution)/shard_map/all_to_all | solution.py:178
  827.8 77.2 %copy-start.3 = (bf16[32,4096]{1,0:T(8,128)(2,1)}, bf16[32,4096]{1,0:T(8,128)(2,1)S(1)}, u32[]{:S(2)}) copy-start(bf16[32,4096]{1,0:T(8,128)(2,1)S(1)} %multiply_convert_fusion) | copy-start | bytes 786436
  831.7 73.3 %copy-start = (bf16[1,4096,256]{2,1,0:T(8,128)(2,1)}, bf16[1,4096,256]{2,1,0:T(8,128)(2,1)S(1)}, u32[]{:S(2)}) copy-start(bf16[1,4096,256]{2,1,0:T(8,128)(2,1)S(1)} %dynamic_update_slice.4) | copy-start | bytes 6291460
Sparse Core Ops, SparseCore 0:
  10.5 84.1 all-gather.6
  96.5 39.2 all-gather.8
  137.6 39.5 all-gather.10
  181.5 204.3 reduce-scatter.2
  388.8 83.5 all-gather.12
  474.1 46.2 all-gather.14
  522.1 56.8 all-gather.16
  590.3 204.0 reduce-scatter.4
